TPU v7x, 512 devices: a whole 4x4x16 slice. The times are simulated.
512 devices in a mesh: seg: 32 (over z_lo, y), blk: 16 (over z_hi, x, core).
Axes of the slice: x: 4, y: 4, z: 16 (z_hi: 2, z_lo: 8; z = z_hi * 8 + z_lo), core: 2. Of those that a mesh axis runs over, the one named last changes fastest.
Arguments:
- queries: float32 [65536, 1024], P(('seg', 'blk')), may hold values from -5 to 5
- keys: float32 [65536, 256], P(('seg', 'blk')), may hold values from -5 to 5
- values: float32 [65536, 256], P(('seg', 'blk')), may hold values from -6 to 6
- gate_logit: float32 [8], replicated, may hold values from -3 to 3
- memory_gain: float32 [1024], replicated, may hold values from 0.5 to 2
Outputs:
- mixed: float32 [65536, 1024], P(('seg', 'blk'))
All inputs are finite; a program needn't handle non-finite values.
Results may differ from a plain program's by a relative error of at most 0.0003.
Values sent between devices are 32-bit elements; how exact they have to be, the bound alone decides.
A program may use at most 64 MiB of HBM per device.

v0:
```python
import jax
import jax.numpy as jnp
from jax import lax
from jax.sharding import PartitionSpec as P

QH = 8
KVH = 2
GROUP = 4
HD = 128


HIGH = lax.Precision.HIGHEST


def side_by_side(arrays, axis, dim, along):
    widths = [a.shape[along] for a in arrays]
    both = jnp.concatenate(arrays, axis=along)
    filled = lax.all_gather(both, axis, axis=dim, tiled=True)
    return tuple(jnp.split(filled, [sum(widths[:k]) for k in range(1, len(widths))], axis=along))


def split_up(shard, dim, peers):
    before, after = (shard.shape[:dim], shard.shape[dim + 1 :])
    return jnp.moveaxis(shard.reshape(*before, peers, -1, *after), dim, 0)


def sent_and_summed(shard, axis, dim):
    peers = lax.axis_size(axis)
    parts = lax.all_to_all(split_up(shard, dim, peers), axis, 0, 0, tiled=True)
    return jnp.sum(parts, axis=0)


def from_everyone(shard, axis):
    copies = jnp.broadcast_to(shard, (lax.axis_size(axis), *shard.shape))
    return lax.all_to_all(copies, axis, split_axis=0, concat_axis=0, tiled=True)


def joined_by_halves(pieces, combine):
    while len(jax.tree.leaves(pieces)[0]) > 1:
        pieces = jax.vmap(combine)(*(pieces[side::2] for side in (0, 1)))
    return pieces[0]


def carried_in(shard, axis, combine, identity):
    peers, index = (lax.axis_size(axis), lax.axis_index(axis))
    passed = jnp.arange(peers) < index

    def kept(part, zero, own):
        part = jnp.where(
            passed.reshape(-1, *(1 for _ in own.shape)), part, jnp.asarray(zero, own.dtype)
        )
        return part

    pieces = from_everyone(shard, axis)
    return joined_by_halves(kept(pieces, identity, shard), combine)


def sigma_map(x):
    return jnp.where(x > 0, x + 1.0, jnp.exp(jnp.minimum(x, 0.0)))


def add_terms(earlier, later):
    return earlier + later


def on_device(queries, keys, values, gate_logit, memory_gain):
    rows = queries.shape[0]
    index = lax.axis_index("blk")
    q_heads = queries.reshape(rows, KVH, GROUP, HD)
    qpos = index * rows + jnp.arange(rows, dtype=jnp.int32)
    scale = 1.0 / jnp.sqrt(jnp.float32(HD))

    def update(carry, pieces):
        top, total, accum = carry
        k_piece, v_piece = pieces
        count = k_piece.shape[0]
        k_h = k_piece.reshape(count, KVH, HD)
        v_h = v_piece.reshape(count, KVH, HD)
        scores = jnp.einsum("rkgd,nkd->kgrn", q_heads, k_h, precision=HIGH) * scale
        kpos = jnp.arange(count, dtype=jnp.int32)
        allowed = (kpos[None, :] <= qpos[:, None])[None, None]
        row_top = jnp.max(jnp.where(allowed, scores, -1e30), axis=-1)
        new_top = jnp.maximum(top, row_top)
        weights = jnp.where(allowed, jnp.exp(scores - new_top[..., None]), 0.0)
        total = jnp.sum(weights, axis=-1)
        accum = jnp.einsum("kgrn,nkd->kgrd", weights, v_h, precision=HIGH)
        return (new_top, total, accum)

    start_state = (
        jnp.full((KVH, GROUP, rows), -1e30, jnp.float32),
        jnp.zeros((KVH, GROUP, rows), jnp.float32),
        jnp.zeros((KVH, GROUP, rows, HD), jnp.float32),
    )
    pieces = side_by_side((keys, values), "blk", 0, 1)
    top, total, accum = lax.cond(
        jnp.int32(0) <= qpos[rows - 1], lambda c: update(c, pieces), lambda c: c, start_state
    )
    attention = accum / total[..., None]
    sig_keys = sigma_map(keys.reshape(rows, KVH, HD))
    partial_value = jnp.einsum(
        "rkd,rke->kde", sig_keys, values.reshape(rows, KVH, HD), precision=HIGH
    ).reshape(KVH * HD, HD)
    shard = sent_and_summed(partial_value, "blk", 0)
    prefix = carried_in(shard, "seg", add_terms, jnp.zeros_like(shard))
    memory = lax.all_gather(prefix, "blk", axis=0, tiled=True)
    retrieval = jnp.einsum(
        "rkgd,kde->kgre", sigma_map(q_heads), memory.reshape(KVH, HD, HD), precision=HIGH
    )
    rms = jnp.sqrt(jnp.mean(retrieval * retrieval, axis=-1, keepdims=True) + 1e-06)
    normed = retrieval / rms * memory_gain.reshape(KVH, GROUP, 1, HD)
    gate = jax.nn.sigmoid(gate_logit).reshape(KVH, GROUP, 1, 1)
    mixed = gate * normed + (1.0 - gate) * attention
    return jnp.transpose(mixed, (2, 0, 1, 3)).reshape(rows, QH * HD)


def solution(mesh):
    return jax.shard_map(
        on_device,
        mesh=mesh,
        in_specs=(
            P(("seg", "blk"), None),
            P(("seg", "blk"), None),
            P(("seg", "blk"), None),
            P(),
            P(),
        ),
        out_specs=P(("seg", "blk"), None),
        check_vma=False,
    )
```

profile of v0, /device:TPU:7, one launch (start us, length us, event | category | flops | bytes accessed | tf_op | source)
XLA Modules:
  0.0 169.5 jit_solution(6998863623988860291)
XLA Ops:
  6.5 0.0 all-gather.3.cloned.1.call-start
  6.5 1.0 copy.19
  7.5 1.0 copy.20
  8.5 0.7 pad_maximum_fusion
  9.3 0.0 all-gather.3.cloned.1.call-update
  9.3 0.9 exponential_select_fusion
  10.2 0.1 copy.34
  10.3 1.2 fusion.19
  11.5 31.8 %all_to_all.10 = f32[16,16,128]{2,1,0:T(8,128)S(1)} all-to-all(f32[16,16,128]{2,1,0:T(8,128)S(1)} %bitcast.56), channel_id=1, replica_groups=mesh['seg'=32,'blk'=16] {'blk'}, dimensions={0} | all-to-all | bytes 262144 | tf_op jit(solution)/shard_map/all_to_all | solution.py:29
  43.3 0.7 broadcast_in_dim.50
  44.1 17.2 %all-to-all-start.1 = ((f32[32,16,128]{2,1,0:T(8,128)}), f32[32,16,128]{2,1,0:T(8,128)S(1)}, u32[]{:S(2)}, u32[]{:S(2)}) async-start(f32[32,16,128]{2,1,0:T(8,128)} %broadcast_in_dim.50), calls=%async_computation.1 | async-start | bytes 524288 | tf_op jit(solution)/shard_map/all_to_all | solution.py:35
  61.3 1.2 copy.16
  62.5 0.6 slice.45
  63.7 0.7 add_divide_fusion
  64.3 0.1 mul.40
  64.4 10.8 %all-to-all-done.1 = f32[32,16,128]{2,1,0:T(8,128)S(1)} async-done(((f32[32,16,128]{2,1,0:T(8,128)}), f32[32,16,128]{2,1,0:T(8,128)S(1)}, u32[]{:S(2)}, u32[]{:S(2)}) %all-to-all-start.1) | async-done | bytes 262176 | tf_op jit(solution)/shard_map/all_to_all | solution.py:35
  75.2 0.1 broadcast_select_fusion
  75.4 49.9 %all-gather = f32[1,256,128]{2,1,0:T(8,128)S(1)} all-gather(f32[1,16,128]{2,1,0:T(8,128)S(1)} %slice_add_fusion.4), channel_id=2, replica_groups=mesh['seg'=32,'blk'=16] {'blk'}, dimensions={1}, use_global_device_ids=true | all-gather | bytes 139264 | tf_op jit(solution)/shard_map/all_gather | solution.py:105
  125.3 0.7 multiply_reduce_fusion
  126.0 17.0 %all-gather.3.cloned.1.call-done = f32[2048,512]{0,1:T(8,128)} async-done(((f32[128,512]{0,1:T(8,128)}), f32[2048,512]{0,1:T(8,128)}) %all-gather.3.cloned.1.call-update) | async-done | bytes 4194320 | tf_op jit(solution)/shard_map/all_gather | solution.py:18
  143.0 0.0 copy-start
  143.0 18.4 %conditional.1 = (f32[2,4,128]{2,1,0:T(4,128)S(1)}, f32[2,4,128,128]{2,3,1,0:T(8,128)S(1)}) conditional(s32[]{:T(128)} %bitcast.12, () %tuple.13, (s32[128]{0:T(128)S(1)}, f32[2048,512]{0,1:T(8,128)}, f32[128,2,4,128]{0,3,2,1:T(8,128)S(1)}) %tuple.25), branch_computations={%region_2.0_spmd, %region_3.6_spmd} | conditional | flops 6463683584 | bytes 39870992 | solution.py:95
  143.0 0.2 iota_compare_fusion
  143.2 2.5 %fusion.24 = (f32[2048,256]{0,1:T(8,128)S(1)}, f32[2048,256]{0,1:T(8,128)S(1)}) fusion(f32[2048,512]{0,1:T(8,128)} %get-tuple-element.15), kind=kLoop, calls=%fused_computation.43 | loop fusion | bytes 8388608 | tf_op jit(solution)/shard_map/split | solution.py:19
  145.7 7.3 %fusion = (f32[2,4,128]{2,1,0:T(4,128)S(1)}, f32[2,2048,128,4]{2,1,3,0:T(8,128)S(1)}) fusion(pred[128,2048]{0,1:T(8,128)(4,1)S(1)} %iota_compare_fusion, f32[2048,2,128,1]{0,2,3,1:T(8,128)S(1)} %bitcast.49, f32[128,2,4,128]{0,3,2,1:T(8,128)S(1)} %get-tuple-element.23), kind=kOutput, calls=%fused_computation.2 | convolution fusion | flops 3227515904 | bytes 11276288 | tf_op jit(solution)/shard_map/cond/branch_1_fun/rkgd,nkd->kgrn/dot_general | solution.py:79
  153.0 6.4 %fusion.3 = f32[2,4,128,128]{2,3,1,0:T(8,128)S(1)} fusion(f32[2048,2,128,1]{0,2,3,1:T(8,128)S(1)} %bitcast.53, f32[2,2048,128,4]{2,1,3,0:T(8,128)S(1)} %get-tuple-element.28, f32[2,4,128]{2,1,0:T(4,128)S(1)} %broadcast_maximum_fusion, pred[128,2048]{0,1:T(8,128)(4,1)S(1)} %iota_compare_fusion), kind=kOutput, calls=%fused_computation.5 | convolution fusion | flops 3227516928 | bytes 11276288 | tf_op jit(solution)/shard_map/cond | solution.py:95
  159.5 1.7 %fusion.5 = f32[2,4,128]{2,1,0:T(4,128)S(1)} fusion(f32[2,2048,128,4]{2,1,3,0:T(8,128)S(1)} %get-tuple-element.28, f32[2,4,128]{2,1,0:T(4,128)S(1)} %broadcast_maximum_fusion, pred[128,2048]{0,1:T(8,128)(4,1)S(1)} %iota_compare_fusion), kind=kLoop, calls=%fused_computation.6 | loop fusion | flops 8387584 | bytes 8658944 | tf_op jit(solution)/shard_map/cond/branch_1_fun/reduce_sum | solution.py:85
  161.4 0.0 copy-done
  161.4 0.2 multiply_add_fusion
  161.7 1.0 copy.23
  (11 shorter events, 0.1 us)
Async XLA Ops:
  6.5 136.4 %all-gather.3.cloned.1.call-start = ((), (), s32[]{:S(2)}) async-start(), calls=%async_computation.2 | async-start | bytes 4456448 | tf_op jit(solution)/shard_map/all_gather | solution.py:18
  44.1 31.1 %all-to-all-start.1 = ((f32[32,16,128]{2,1,0:T(8,128)}), f32[32,16,128]{2,1,0:T(8,128)S(1)}, u32[]{:S(2)}, u32[]{:S(2)}) async-start(f32[32,16,128]{2,1,0:T(8,128)} %broadcast_in_dim.50), calls=%async_computation.1 | async-start | bytes 524288 | tf_op jit(solution)/shard_map/all_to_all | solution.py:35
  143.0 18.5 %copy-start = (f32[1024]{0:T(1024)S(1)}, f32[1024]{0:T(1024)}, u32[]{:S(2)}) copy-start(f32[1024]{0:T(1024)} %param.11) | copy-start | bytes 12292
Sparse Core Ops, SparseCore 0:
  10.5 132.4 all-gather.2
where the time goes:
time: 170 us
  blocking collectives  81.7 us (48%)
  waiting for transfers between devices  27.8 us (16%)
  starting transfers between devices  17.2 us (10%)
  matrix products  15.6 us (9%)
  between operations  14.1 us (8%)
  local copies, waits for them, and re-layouts  8.18 us (5%)
  other arithmetic  4.63 us (3%)
    all_gather x1, blocking collectives, on_device(): memory = lax.all_gather(prefix, 'blk', axis=0, tiled=True)  49.9 us
    all_to_all x1, blocking collectives, sent_and_summed(): parts = lax.all_to_all(split_up(shard, dim, peers), axis, 0, 0, tiled=True)  31.8 us
    all_to_all x1, starting transfers between devices, from_everyone(): return lax.all_to_all(copies, axis, split_axis=0, concat_axis=0, tiled=True)  17.2 us
    all_gather x1, waiting for transfers between devices, side_by_side(): filled = lax.all_gather(both, axis, axis=dim, tiled=True)  17 us
    all_to_all x1, waiting for transfers between devices, from_everyone(): return lax.all_to_all(copies, axis, split_axis=0, concat_axis=0, tiled=True)  10.8 us
    dot_general x1, matrix products, update(): scores = jnp.einsum('rkgd,nkd->kgrn', q_heads, k_h, precision=HIGH) * scale  7.34 us
    cond x1, matrix products, on_device(): lax.cond(jnp.int32(0) <= qpos[rows - 1], lambda c: update(c, pieces), lam...  6.44 us
  transfers between devices with their start and end apart: 2, of which 2 were waited for; matrix products, arithmetic and copies ran while one was open for 4% of the time, Pallas kernels for 0%

commit v1 on v0

v1 whole, which is shorter than its diff:
```python
import jax
import jax.numpy as jnp
from jax import lax
from jax.experimental import pallas as pl
from jax.experimental.pallas import tpu as pltpu
from jax.sharding import PartitionSpec as P

KVH = 2
GROUP = 4
HD = 128
NX = 4
NY = 4
NZ = 8
NCH = 4
LOG2E = 1.4426950408889634
MASKED = -1e30
MESH = pl.DeviceIdType.MESH
HIGH = lax.Precision.HIGHEST
NT = (((1,), (1,)), ((), ()))
TN = (((0,), (0,)), ((), ()))
NN = (((1,), (0,)), ((), ()))


def sigma_map(x):
    return jnp.where(x > 0, x + 1.0, jnp.exp(jnp.minimum(x, 0.0)))


def halves(x):
    top = x.astype(jnp.bfloat16)
    return top, (x - top.astype(jnp.float32)).astype(jnp.bfloat16)


def mm(a, b, dims):
    return lax.dot_general(a, b, dims, preferred_element_type=jnp.float32)


def kernel(
    q_hbm,
    k_hbm,
    v_hbm,
    gate_ref,
    gain_ref,
    o_ref,
    q_ref,
    kv_ref,
    qs_ref,
    m_ref,
    l_ref,
    acc_ref,
    partial_ref,
    parts_ref,
    shard_ref,
    ypart_ref,
    total_ref,
    zpart_ref,
    other_ref,
    stage_ref,
    own_ref,
    memory_ref,
    load_sem,
    zs,
    zr,
    xs,
    xr,
    ss,
    sr,
    ps,
    pr,
    ys,
    yr,
    ts,
    tr,
    fs,
    fr,
    ms,
    mr,
    gs,
    gr,
):
    seg = lax.axis_index("seg")
    blk = lax.axis_index("blk")
    z_lo = lax.div(seg, NY)
    y = lax.rem(seg, NY)
    z_hi = lax.div(blk, 2 * NX)
    j = lax.rem(blk, 2 * NX)
    x = lax.div(j, 2)
    c = lax.rem(j, 2)
    rows = q_ref.shape[0]
    step = rows // NCH

    def at(zh, zl, xx, yy, cc):
        return {"seg": zl * NY + yy, "blk": zh * 2 * NX + xx * 2 + cc}

    def near(dx, dc):
        return at(z_hi, z_lo, lax.rem(x + dx, NX), y, lax.rem(c + dc, 2))

    def along_y(dy):
        return at(z_hi, z_lo, x, lax.rem(y + dy, NY), c)

    def remote(src, dst, send, recv, device):
        return pltpu.make_async_remote_copy(
            src_ref=src,
            dst_ref=dst,
            send_sem=send,
            recv_sem=recv,
            device_id=device,
            device_id_type=MESH,
        )

    others = [(dx, dc) for dx in range(NX) for dc in range(2) if (dx, dc) != (0, 0)]

    loads = [
        pltpu.make_async_copy(
            hbm.at[pl.ds(ch * step, step)], kv_ref.at[0, ch, c, x, kv], load_sem.at[kv, ch]
        )
        for ch in range(NCH)
        for kv, hbm in enumerate((k_hbm, v_hbm))
    ]
    q_load = pltpu.make_async_copy(q_hbm, q_ref, load_sem.at[2, 0])
    for load in loads:
        load.start()
    q_load.start()
    zpart_ref[...] = jnp.zeros_like(zpart_ref)

    barrier = pltpu.get_barrier_semaphore()
    opposite = at(1 - z_hi, z_lo, x, y, c)
    greeted = [near(dx, dc) for dx, dc in others]
    greeted += [along_y(dy) for dy in range(1, NY)]
    greeted += [opposite]
    for d in range(1, NZ):
        for e in range(2):
            greeted.append(at(lax.rem(z_hi + e, 2), lax.rem(z_lo + d, NZ), x, y, c))
    for device in greeted:
        pl.semaphore_signal(barrier, inc=1, device_id=device, device_id_type=MESH)

    for load in loads:
        load.wait()
    for k in range(KVH):
        cols = pl.ds(k * HD, HD)
        key = kv_ref[0, :, c, x, 0, :, cols].reshape(rows, HD)
        value = kv_ref[0, :, c, x, 1, :, cols].reshape(rows, HD)
        partial_ref[pl.ds(k * 4, 4)] = lax.dot_general(
            sigma_map(key), value, TN, precision=HIGH, preferred_element_type=jnp.float32
        ).reshape(4, 32, HD)
    q_load.wait()
    scale = LOG2E / (HD**0.5)
    for k in range(KVH):
        for g in range(GROUP):
            h = k * GROUP + g
            top, low = halves(q_ref[:, pl.ds(h * HD, HD)] * scale)
            qs_ref[k, pl.ds(g * rows, rows), pl.ds(0, HD)] = top
            qs_ref[k, pl.ds(g * rows, rows), pl.ds(HD, HD)] = low
    m_ref[...] = jnp.full_like(m_ref, MASKED)
    l_ref[...] = jnp.zeros_like(l_ref)
    acc_ref[...] = jnp.zeros_like(acc_ref)

    pl.semaphore_wait(barrier, len(greeted))

    def across(ch):
        return remote(
            kv_ref.at[0, ch, c, x], kv_ref.at[1, ch, c, x], zs.at[ch], zr.at[ch], opposite
        )

    def spread(half, ch, dx):
        item = kv_ref.at[half, ch, c, x]
        return remote(
            item, item, xs.at[half, ch, dx - 1], xr.at[half, ch, dx - 1], near(dx, 0)
        )

    def share(half, ch, dx):
        item = kv_ref.at[half, ch, c, lax.rem(x + NX - dx, NX)]
        return remote(item, item, ss.at[half, ch, dx], sr.at[half, ch, dx], near(0, 1))

    @pl.when(z_hi == 0)
    def _():
        for ch in range(NCH):
            across(ch).start()

    def scatter(n):
        dx, dc = others[n]
        target = lax.rem(x + dx, NX) * 2 + lax.rem(c + dc, 2)
        return remote(
            partial_ref.at[target], parts_ref.at[j], ps.at[n], pr.at[n], near(dx, dc)
        )

    for n in range(len(others)):
        scatter(n).start()
    parts_ref[j] = partial_ref[j]

    def begin(half, ch):
        for dx in range(1, NX):
            spread(half, ch, dx).start()
        share(half, ch, 0).start()

    def pass_on(half, ch):
        for dx in range(1, NX):
            spread(half, ch, dx).wait_recv()
            share(half, ch, dx).start()

    def arrive(half, ch):
        for dx in range(NX):
            share(half, ch, dx).wait_recv()

    @pl.loop(0, NCH)
    def _(ch):
        begin(0, ch)

    for n in range(len(others)):
        scatter(n).wait_recv()
    shard_ref[...] = jnp.sum(parts_ref[...], axis=0).reshape(NY, 8, HD)

    def turn(dy):
        return remote(
            shard_ref.at[lax.rem(y + dy, NY)],
            ypart_ref.at[y],
            ys.at[dy - 1],
            yr.at[dy - 1],
            along_y(dy),
        )

    for dy in range(1, NY):
        turn(dy).start()
    ypart_ref[y] = shard_ref[y]

    @pl.loop(0, NCH)
    def _(ch):
        pass_on(0, ch)

    for dy in range(1, NY):
        turn(dy).wait_recv()
    total_ref[...] = jnp.sum(ypart_ref[...], axis=0)

    def onward(d, e):
        return remote(
            total_ref,
            zpart_ref.at[d - 1, e],
            ts.at[d - 1, e],
            tr.at[d - 1, e],
            at(lax.rem(z_hi + e, 2), lax.rem(z_lo + d, NZ), x, y, c),
        )

    over = remote(ypart_ref, other_ref, fs, fr, opposite)
    over.start()
    for d in range(1, NZ):

        @pl.when(z_lo + d < NZ)
        def _(d=d):
            for e in range(2):
                onward(d, e).start()

    qpos = j * rows + lax.rem(
        lax.broadcasted_iota(jnp.int32, (GROUP * rows, 2 * HD), 0), rows
    )
    slot = lax.broadcasted_iota(jnp.int32, (GROUP * rows, 2 * HD), 1)
    per = NX * step
    base_kpos = (
        lax.rem(lax.div(slot, step), NX) * 2 + lax.div(slot, per)
    ) * rows + lax.rem(slot, step)

    def attend(half, ch):
        for k in range(KVH):
            cols = pl.ds(k * HD, HD)
            key = kv_ref[half, ch, :, :, 0, :, cols].reshape(2 * NX * step, HD)
            value = kv_ref[half, ch, :, :, 1, :, cols].reshape(2 * NX * step, HD)
            k_top, k_low = halves(key)
            v_both = jnp.concatenate(halves(value), axis=1)
            q_both = qs_ref[k]
            scores = mm(q_both, jnp.concatenate((k_top, k_top), axis=1), NT)
            scores += mm(qs_ref[k, :, pl.ds(0, HD)], k_low, NT)
            if half == 0:
                scores = jnp.where(base_kpos + ch * step <= qpos, scores, MASKED)
            old = m_ref[k]
            new = jnp.maximum(old, jnp.max(scores, axis=1, keepdims=True))
            m_ref[k] = new
            decay = jnp.exp2(old - new)
            weights = jnp.exp2(scores - jnp.concatenate((new, new), axis=1))
            l_ref[k] = l_ref[k] * decay + weights[:, :HD] + weights[:, HD:]
            w_top, w_low = halves(weights)
            both = mm(w_top, v_both, NN) + mm(w_low, v_both, NN)
            acc_ref[k] = acc_ref[k] * decay + both[:, :HD] + both[:, HD:]

    @pl.loop(0, NCH)
    def _(ch):
        arrive(0, ch)
        attend(0, ch)

    for d in range(1, NZ):

        @pl.when(z_lo >= d)
        def _(d=d):
            for e in range(2):
                onward(d, e).wait_recv()

    over.wait_recv()
    carried = jnp.sum(zpart_ref[...], axis=(0, 1))
    for row in range(NY):
        stage_ref[row] = carried
        carried = carried + ypart_ref[row] + other_ref[row]

    def back(dy):
        return remote(
            stage_ref.at[lax.rem(y + dy, NY)],
            own_ref.at[y],
            ms.at[dy - 1],
            mr.at[dy - 1],
            along_y(dy),
        )

    for dy in range(1, NY):
        back(dy).start()
    own_ref[y] = stage_ref[y]
    for dy in range(1, NY):
        back(dy).wait_recv()

    def gather(n):
        dx, dc = others[n]
        return remote(own_ref, memory_ref.at[j], gs.at[n], gr.at[n], near(dx, dc))

    for n in range(len(others)):
        gather(n).start()
    memory_ref[j] = own_ref[...]
    for n in range(len(others)):
        gather(n).wait_recv()

    gates = 1.0 / (1.0 + jnp.exp(-gate_ref[...]))
    for k in range(KVH):
        memory = memory_ref[pl.ds(k * 4, 4)].reshape(HD, HD)
        for g in range(GROUP):
            h = k * GROUP + g
            cols = pl.ds(h * HD, HD)
            got = lax.dot_general(
                sigma_map(q_ref[:, cols]),
                memory,
                NN,
                precision=HIGH,
                preferred_element_type=jnp.float32,
            )
            rms = jnp.sqrt(jnp.mean(got * got, axis=1, keepdims=True) + 1e-6)
            gate = gates[:, h : h + 1]
            o_ref[:, cols] = (got / rms) * (gain_ref[h : h + 1, :] * gate)

    @pl.when(z_hi == 1)
    def _():
        @pl.loop(0, NCH)
        def _(ch):
            across(ch).wait_recv()
            begin(1, ch)
            pass_on(1, ch)
            arrive(1, ch)
            attend(1, ch)

        @pl.loop(0, NCH)
        def _(ch):
            for dx in range(1, NX):
                spread(1, ch, dx).wait_send()
            for dx in range(NX):
                share(1, ch, dx).wait_send()

    for k in range(KVH):
        for g in range(GROUP):
            h = k * GROUP + g
            cols = pl.ds(h * HD, HD)
            part = pl.ds(g * rows, rows)
            total = jnp.sum(l_ref[k, part], axis=1, keepdims=True)
            gate = gates[:, h : h + 1]
            o_ref[:, cols] += acc_ref[k, part] * ((1.0 - gate) / total)

    @pl.when(z_hi == 0)
    def _():
        for ch in range(NCH):
            across(ch).wait_send()

    @pl.loop(0, NCH)
    def _(ch):
        for dx in range(1, NX):
            spread(0, ch, dx).wait_send()
        for dx in range(NX):
            share(0, ch, dx).wait_send()

    for n in range(len(others)):
        scatter(n).wait_send()
        gather(n).wait_send()
    for dy in range(1, NY):
        turn(dy).wait_send()
        back(dy).wait_send()
    over.wait_send()
    for d in range(1, NZ):

        @pl.when(z_lo + d < NZ)
        def _(d=d):
            for e in range(2):
                onward(d, e).wait_send()


def on_device(queries, keys, values, gate_logit, memory_gain):
    rows = queries.shape[0]
    heads = KVH * GROUP
    f32 = jnp.float32
    sem = pltpu.SemaphoreType.DMA
    peers = 2 * NX - 1
    return pl.pallas_call(
        kernel,
        out_shape=jax.ShapeDtypeStruct((rows, heads * HD), f32),
        in_specs=[pl.BlockSpec(memory_space=pl.ANY)] * 3
        + [pl.BlockSpec(memory_space=pltpu.VMEM)] * 2,
        out_specs=pl.BlockSpec(memory_space=pltpu.VMEM),
        scratch_shapes=[
            pltpu.VMEM((rows, heads * HD), f32),
            pltpu.VMEM((2, NCH, 2, NX, 2, rows // NCH, KVH * HD), f32),
            pltpu.VMEM((KVH, GROUP * rows, 2 * HD), jnp.bfloat16),
            pltpu.VMEM((KVH, GROUP * rows, HD), f32),
            pltpu.VMEM((KVH, GROUP * rows, HD), f32),
            pltpu.VMEM((KVH, GROUP * rows, HD), f32),
            pltpu.VMEM((2 * NX, 32, HD), f32),
            pltpu.VMEM((2 * NX, 32, HD), f32),
            pltpu.VMEM((NY, 8, HD), f32),
            pltpu.VMEM((NY, 8, HD), f32),
            pltpu.VMEM((8, HD), f32),
            pltpu.VMEM((NZ - 1, 2, 8, HD), f32),
            pltpu.VMEM((NY, 8, HD), f32),
            pltpu.VMEM((NY, 8, HD), f32),
            pltpu.VMEM((NY, 8, HD), f32),
            pltpu.VMEM((2 * NX, NY, 8, HD), f32),
            sem((3, NCH)),
            sem((NCH,)),
            sem((NCH,)),
            sem((2, NCH, NX - 1)),
            sem((2, NCH, NX - 1)),
            sem((2, NCH, NX)),
            sem((2, NCH, NX)),
            sem((peers,)),
            sem((peers,)),
            sem((NY - 1,)),
            sem((NY - 1,)),
            sem((NZ - 1, 2)),
            sem((NZ - 1, 2)),
            sem,
            sem,
            sem((NY - 1,)),
            sem((NY - 1,)),
            sem((peers,)),
            sem((peers,)),
        ],
        compiler_params=pltpu.CompilerParams(collective_id=0, has_side_effects=True),
    )(
        queries,
        keys,
        values,
        gate_logit.reshape(1, heads),
        memory_gain.reshape(heads, HD),
    )


def solution(mesh):
    return jax.shard_map(
        on_device,
        mesh=mesh,
        in_specs=(
            P(("seg", "blk"), None),
            P(("seg", "blk"), None),
            P(("seg", "blk"), None),
            P(),
            P(),
        ),
        out_specs=P(("seg", "blk"), None),
        check_vma=False,
    )
```

time: 170 us -> 86.1 us (0.51)
  the two profiles are of different devices: /device:TPU:7 before, /device:TPU:289 now
where the time goes in v1:
time: 86.1 us; the launch traced here: 85.9 us
  Pallas kernels  84 us (98%)
  local copies, waits for them, and re-layouts  1.89 us (2%)
    pallas_call x1, Pallas kernels, on_device(): pl.pallas_call(kernel, out_shape=jax.ShapeDtypeStruct((rows, heads * HD),...  84 us
    unnamed x1, local copies, waits for them, and re-layouts  1.89 us

profile of v1, /device:TPU:289, one launch (start us, length us, event | category | flops | bytes accessed | tf_op | source)
XLA Modules:
  0.0 85.9 jit_solution(1785080038739341417)
XLA Ops:
  0.0 84.0 %shard_map.55 = f32[128,1024]{1,0:T(8,128)} custom-call(f32[128,1024]{1,0:T(8,128)} %q_hbm.1, f32[128,256]{1,0:T(8,128)} %k_hbm.1, f32[128,256]{1,0:T(8,128)} %v_hbm.1, f32[1,8]{1,0:T(1,128)} %bitcast.3, f32[8,128]{1,0:T(8,128)} %bitcast.2), custom_call_target="tpu_custom_call" | custom-call | tf_op jit(solution)/shard_map/pallas_call | solution.py:401
  84.0 1.9 %copy.7 = f32[128,1024]{1,0:T(8,128)} copy(f32[128,1024]{1,0:T(8,128)} %shard_map.55) | data formatting | bytes 1048576

commit v2 on v1

--- a/solution.py
+++ b/solution.py
@@ -171,7 +171,9 @@
         item = kv_ref.at[half, ch, c, lax.rem(x + NX - dx, NX)]
         return remote(item, item, ss.at[half, ch, dx], sr.at[half, ch, dx], near(0, 1))
 
-    @pl.when(z_hi == 0)
+    nearest = (z_lo == 0) | (z_lo == NZ - 1)
+
+    @pl.when((z_hi == 0) & nearest)
     def _():
         for ch in range(NCH):
             across(ch).start()
@@ -221,11 +223,6 @@
     for dy in range(1, NY):
         turn(dy).start()
     ypart_ref[y] = shard_ref[y]
-
-    @pl.loop(0, NCH)
-    def _(ch):
-        pass_on(0, ch)
-
     for dy in range(1, NY):
         turn(dy).wait_recv()
     total_ref[...] = jnp.sum(ypart_ref[...], axis=0)
@@ -247,6 +244,15 @@
         def _(d=d):
             for e in range(2):
                 onward(d, e).start()
+
+    @pl.when((z_hi == 0) & jnp.logical_not(nearest))
+    def _():
+        for ch in range(NCH):
+            across(ch).start()
+
+    @pl.loop(0, NCH)
+    def _(ch):
+        pass_on(0, ch)
 
     qpos = j * rows + lax.rem(
         lax.broadcasted_iota(jnp.int32, (GROUP * rows, 2 * HD), 0), rows
@@ -279,23 +285,11 @@
             both = mm(w_top, v_both, NN) + mm(w_low, v_both, NN)
             acc_ref[k] = acc_ref[k] * decay + both[:, :HD] + both[:, HD:]
 
-    @pl.loop(0, NCH)
-    def _(ch):
-        arrive(0, ch)
-        attend(0, ch)
-
-    for d in range(1, NZ):
-
-        @pl.when(z_lo >= d)
-        def _(d=d):
-            for e in range(2):
-                onward(d, e).wait_recv()
-
-    over.wait_recv()
-    carried = jnp.sum(zpart_ref[...], axis=(0, 1))
-    for row in range(NY):
-        stage_ref[row] = carried
-        carried = carried + ypart_ref[row] + other_ref[row]
+    def attend_near(start, stop):
+        @pl.loop(start, stop)
+        def _(ch):
+            arrive(0, ch)
+            attend(0, ch)
 
     def back(dy):
         return remote(
@@ -306,49 +300,86 @@
             along_y(dy),
         )
 
-    for dy in range(1, NY):
-        back(dy).start()
-    own_ref[y] = stage_ref[y]
-    for dy in range(1, NY):
-        back(dy).wait_recv()
-
     def gather(n):
         dx, dc = others[n]
         return remote(own_ref, memory_ref.at[j], gs.at[n], gr.at[n], near(dx, dc))
 
-    for n in range(len(others)):
-        gather(n).start()
-    memory_ref[j] = own_ref[...]
-    for n in range(len(others)):
-        gather(n).wait_recv()
+    def carry():
+        for d in range(1, NZ):
+
+            @pl.when(z_lo >= d)
+            def _(d=d):
+                for e in range(2):
+                    onward(d, e).wait_recv()
+
+        over.wait_recv()
+        carried = jnp.sum(zpart_ref[...], axis=(0, 1))
+        for row in range(NY):
+            stage_ref[row] = carried
+            carried = carried + ypart_ref[row] + other_ref[row]
+        for dy in range(1, NY):
+            back(dy).start()
+        own_ref[y] = stage_ref[y]
+
+    def collect():
+        for dy in range(1, NY):
+            back(dy).wait_recv()
+        for n in range(len(others)):
+            gather(n).start()
+        memory_ref[j] = own_ref[...]
 
     gates = 1.0 / (1.0 + jnp.exp(-gate_ref[...]))
-    for k in range(KVH):
-        memory = memory_ref[pl.ds(k * 4, 4)].reshape(HD, HD)
-        for g in range(GROUP):
-            h = k * GROUP + g
-            cols = pl.ds(h * HD, HD)
-            got = lax.dot_general(
-                sigma_map(q_ref[:, cols]),
-                memory,
-                NN,
-                precision=HIGH,
-                preferred_element_type=jnp.float32,
-            )
-            rms = jnp.sqrt(jnp.mean(got * got, axis=1, keepdims=True) + 1e-6)
-            gate = gates[:, h : h + 1]
-            o_ref[:, cols] = (got / rms) * (gain_ref[h : h + 1, :] * gate)
+
+    def retrieve():
+        for n in range(len(others)):
+            gather(n).wait_recv()
+        for k in range(KVH):
+            memory = memory_ref[pl.ds(k * 4, 4)].reshape(HD, HD)
+            for g in range(GROUP):
+                h = k * GROUP + g
+                cols = pl.ds(h * HD, HD)
+                got = lax.dot_general(
+                    sigma_map(q_ref[:, cols]),
+                    memory,
+                    NN,
+                    precision=HIGH,
+                    preferred_element_type=jnp.float32,
+                )
+                rms = jnp.sqrt(jnp.mean(got * got, axis=1, keepdims=True) + 1e-6)
+                gate = gates[:, h : h + 1]
+                o_ref[:, cols] = (got / rms) * (gain_ref[h : h + 1, :] * gate)
+
+    @pl.when(z_hi == 0)
+    def _():
+        attend_near(0, NCH)
+        carry()
+        collect()
+        retrieve()
 
     @pl.when(z_hi == 1)
     def _():
-        @pl.loop(0, NCH)
-        def _(ch):
+        attend_near(0, NCH)
+        for ch in range(NCH):
             across(ch).wait_recv()
             begin(1, ch)
-            pass_on(1, ch)
-            arrive(1, ch)
-            attend(1, ch)
-
+        pass_on(1, 0)
+        pass_on(1, 1)
+        arrive(1, 0)
+        attend(1, 0)
+        carry()
+        pass_on(1, 2)
+        arrive(1, 1)
+        attend(1, 1)
+        collect()
+        pass_on(1, 3)
+        arrive(1, 2)
+        attend(1, 2)
+        retrieve()
+        arrive(1, 3)
+        attend(1, 3)
+
+    @pl.when(z_hi == 1)
+    def _():
         @pl.loop(0, NCH)
         def _(ch):
             for dx in range(1, NX):

time: 86.1 us -> 64.3 us (0.75)
  Pallas kernels: 84 us -> 62.2 us
    pallas_call x1, Pallas kernels: 84 us -> 62.2 us  [on_device(): pl.pallas_call(kernel, out_shape=jax.ShapeDtypeStruct((rows, heads * HD),...]
where the time goes in v2:
time: 64.3 us; the launch traced here: 64.1 us
  Pallas kernels  62.2 us (97%)
  local copies, waits for them, and re-layouts  1.89 us (3%)
    pallas_call x1, Pallas kernels, on_device(): pl.pallas_call(kernel, out_shape=jax.ShapeDtypeStruct((rows, heads * HD),...  62.2 us
    unnamed x1, local copies, waits for them, and re-layouts  1.89 us

profile of v2, /device:TPU:289, one launch (start us, length us, event | category | flops | bytes accessed | tf_op | source)
XLA Modules:
  0.0 64.1 jit_solution(835921295749174559)
XLA Ops:
  0.0 62.2 %shard_map.55 = f32[128,1024]{1,0:T(8,128)} custom-call(f32[128,1024]{1,0:T(8,128)} %q_hbm.1, f32[128,256]{1,0:T(8,128)} %k_hbm.1, f32[128,256]{1,0:T(8,128)} %v_hbm.1, f32[1,8]{1,0:T(1,128)} %bitcast.3, f32[8,128]{1,0:T(8,128)} %bitcast.2), custom_call_target="tpu_custom_call" | custom-call | tf_op jit(solution)/shard_map/pallas_call | solution.py:432
  62.2 1.9 %copy.7 = f32[128,1024]{1,0:T(8,128)} copy(f32[128,1024]{1,0:T(8,128)} %shard_map.55) | data formatting | bytes 1048576

commit v3 on v2

--- a/solution.py
+++ b/solution.py
@@ -171,9 +171,7 @@
         item = kv_ref.at[half, ch, c, lax.rem(x + NX - dx, NX)]
         return remote(item, item, ss.at[half, ch, dx], sr.at[half, ch, dx], near(0, 1))
 
-    nearest = (z_lo == 0) | (z_lo == NZ - 1)
-
-    @pl.when((z_hi == 0) & nearest)
+    @pl.when(z_hi == 0)
     def _():
         for ch in range(NCH):
             across(ch).start()
@@ -244,11 +242,6 @@
         def _(d=d):
             for e in range(2):
                 onward(d, e).start()
-
-    @pl.when((z_hi == 0) & jnp.logical_not(nearest))
-    def _():
-        for ch in range(NCH):
-            across(ch).start()
 
     @pl.loop(0, NCH)
     def _(ch):
@@ -364,13 +357,13 @@
             begin(1, ch)
         pass_on(1, 0)
         pass_on(1, 1)
+        carry()
         arrive(1, 0)
         attend(1, 0)
-        carry()
         pass_on(1, 2)
+        collect()
         arrive(1, 1)
         attend(1, 1)
-        collect()
         pass_on(1, 3)
         arrive(1, 2)
         attend(1, 2)

time: 64.3 us -> 60.6 us (0.942)
  Pallas kernels: 62.2 us -> 58.5 us
    pallas_call x1, Pallas kernels: 62.2 us -> 58.5 us  [on_device(): pl.pallas_call(kernel, out_shape=jax.ShapeDtypeStruct((rows, heads * HD),...]
where the time goes in v3:
time: 60.6 us; the launch traced here: 60.4 us
  Pallas kernels  58.5 us (97%)
  local copies, waits for them, and re-layouts  1.89 us (3%)
    pallas_call x1, Pallas kernels, on_device(): pl.pallas_call(kernel, out_shape=jax.ShapeDtypeStruct((rows, heads * HD),...  58.5 us
    unnamed x1, local copies, waits for them, and re-layouts  1.89 us

profile of v3, /device:TPU:289, one launch (start us, length us, event | category | flops | bytes accessed | tf_op | source)
XLA Modules:
  0.0 60.4 jit_solution(1184798169404125996)
XLA Ops:
  0.0 58.5 %shard_map.55 = f32[128,1024]{1,0:T(8,128)} custom-call(f32[128,1024]{1,0:T(8,128)} %q_hbm.1, f32[128,256]{1,0:T(8,128)} %k_hbm.1, f32[128,256]{1,0:T(8,128)} %v_hbm.1, f32[1,8]{1,0:T(1,128)} %bitcast.3, f32[8,128]{1,0:T(8,128)} %bitcast.2), custom_call_target="tpu_custom_call" | custom-call | tf_op jit(solution)/shard_map/pallas_call | solution.py:425
  58.5 1.9 %copy.7 = f32[128,1024]{1,0:T(8,128)} copy(f32[128,1024]{1,0:T(8,128)} %shard_map.55) | data formatting | bytes 1048576

commit v4 on v3

--- a/solution.py
+++ b/solution.py
@@ -188,12 +188,12 @@
     parts_ref[j] = partial_ref[j]
 
     def begin(half, ch):
-        for dx in range(1, NX):
+        for dx in (1, 3, 2):
             spread(half, ch, dx).start()
         share(half, ch, 0).start()
 
     def pass_on(half, ch):
-        for dx in range(1, NX):
+        for dx in (1, 3, 2):
             spread(half, ch, dx).wait_recv()
             share(half, ch, dx).start()
 
@@ -358,13 +358,13 @@
         pass_on(1, 0)
         pass_on(1, 1)
         carry()
+        pass_on(1, 2)
         arrive(1, 0)
         attend(1, 0)
-        pass_on(1, 2)
         collect()
+        pass_on(1, 3)
         arrive(1, 1)
         attend(1, 1)
-        pass_on(1, 3)
         arrive(1, 2)
         attend(1, 2)
         retrieve()

time: 60.6 us -> 60.3 us (level)
  no operation moved by 1% of the time
where the time goes in v4:
time: 60.3 us; the launch traced here: 60.1 us
  Pallas kernels  58.2 us (97%)
  local copies, waits for them, and re-layouts  1.89 us (3%)
    pallas_call x1, Pallas kernels, on_device(): pl.pallas_call(kernel, out_shape=jax.ShapeDtypeStruct((rows, heads * HD),...  58.2 us
    unnamed x1, local copies, waits for them, and re-layouts  1.89 us

profile of v4, /device:TPU:289, one launch (start us, length us, event | category | flops | bytes accessed | tf_op | source)
XLA Modules:
  0.0 60.1 jit_solution(16436220235460722307)
XLA Ops:
  0.0 58.2 %shard_map.55 = f32[128,1024]{1,0:T(8,128)} custom-call(f32[128,1024]{1,0:T(8,128)} %q_hbm.1, f32[128,256]{1,0:T(8,128)} %k_hbm.1, f32[128,256]{1,0:T(8,128)} %v_hbm.1, f32[1,8]{1,0:T(1,128)} %bitcast.3, f32[8,128]{1,0:T(8,128)} %bitcast.2), custom_call_target="tpu_custom_call" | custom-call | tf_op jit(solution)/shard_map/pallas_call | solution.py:425
  58.2 1.9 %copy.7 = f32[128,1024]{1,0:T(8,128)} copy(f32[128,1024]{1,0:T(8,128)} %shard_map.55) | data formatting | bytes 1048576
